TPU v7x, 128 devices: a whole 4x4x4 slice. The times are simulated.
128 devices in a mesh: row: 8 (over x, y_hi), col: 16 (over y_lo, z, core).
Axes of the slice: x: 4, y: 4 (y_hi: 2, y_lo: 2; y = y_hi * 2 + y_lo), z: 4, core: 2. Of those that a mesh axis runs over, the one named last changes fastest.
Arguments:
- front_trailing: float32 [16384, 16384], P('row', 'col'), may hold values from -6 to 6
- panel_columns: float32 [16384, 1024], P('row', 'col'), may hold values from -0.1875 to 0.1875
- panel_rows: float32 [1024, 16384], P('row', 'col'), may hold values from -6 to 6
- pivots: int32 [1024], replicated, may hold values from 0 to 1023, each once
- diag_inverse: float32 [1024, 1024], replicated, may hold values from -0.1875 to 0.1875
- test_matrix: float32 [16384, 512], P('col'), may hold values from -0.046875 to 0.046875
Outputs:
- schur: float32 [16384, 16384], P('row', 'col')
- off_samples: float32 [16384, 512], P(('row', 'col'))
- leaf_blocks: float32 [16384, 128], P(('row', 'col'))
- group_gram: float32 [8, 512, 512], P('row')
Inputs may be any that keep to these rules, and one draw needn't show every extreme that they name: pivots names each of 0 to 1023 once.
All inputs are finite; a program needn't handle non-finite values.
Results may differ from a plain program's by a relative error of at most 0.000084.
Values sent between devices are 32-bit elements; how exact they have to be, the bound alone decides.
A program may use at most 128 MiB of HBM per device.

v0:
```python
import jax
import jax.numpy as jnp
from jax import lax
from jax.sharding import PartitionSpec as P

LEAF = 128


def product(left, right):
    return jnp.dot(left, right, precision=lax.Precision.HIGH, preferred_element_type=jnp.float32)


def body(front_trailing, panel_columns, panel_rows, pivots, diag_inverse, test_matrix):
    col_count = lax.axis_size("col")
    row_count = lax.axis_size("row")
    row_index = lax.axis_index("row")
    col_index = lax.axis_index("col")
    height, width = front_trailing.shape
    upper_full = lax.all_gather(panel_rows, "row", axis=0, tiled=True)
    left = lax.all_gather(panel_columns, "col", axis=1, tiled=True)
    upper = jnp.take(upper_full, pivots, axis=0)
    weight = product(diag_inverse, upper)
    schur = front_trailing - product(left, weight)
    rows = row_index * height + jnp.arange(height, dtype=jnp.int32)
    cols = col_index * width + jnp.arange(width, dtype=jnp.int32)
    same_leaf = rows[:, None] // LEAF == cols[None, :] // LEAF
    masked = jnp.where(same_leaf, jnp.zeros_like(schur), schur)
    partial = product(masked, test_matrix)
    count = width // LEAF
    ratio = col_count // row_count
    leaves = height // LEAF
    kept = []
    for leaf in range(leaves):
        held = col_index == row_index * ratio + leaf // count
        block = schur[
            leaf * LEAF : (leaf + 1) * LEAF, leaf % count * LEAF : (leaf % count + 1) * LEAF
        ]
        kept.append(jnp.where(held, block, jnp.zeros_like(block)))
    both = jnp.concatenate([partial, jnp.concatenate(kept, axis=0)], axis=1)
    own = lax.psum_scatter(both, "col", scatter_dimension=0, tiled=True)
    own_samples = own[:, : partial.shape[1]]
    leaf_blocks = own[:, partial.shape[1] :]
    gram = lax.dot_general(
        own_samples,
        own_samples,
        (((0,), (0,)), ((), ())),
        precision=lax.Precision.HIGH,
        preferred_element_type=jnp.float32,
    )
    gram = lax.psum(gram, "col")
    route = [(i, i ^ 1) for i in range(row_count)]
    gram = gram + lax.ppermute(gram, "row", route)
    group_gram = (gram / (2 * height))[None]
    return (schur, own_samples, leaf_blocks, group_gram)


def solution(mesh):
    placed = (P("row", "col"), P("row", "col"), P("row", "col"), P(), P(), P("col", None))
    return jax.shard_map(
        body,
        mesh=mesh,
        in_specs=placed,
        out_specs=(
            P("row", "col"),
            P(("row", "col"), None),
            P(("row", "col"), None),
            P("row", None, None),
        ),
        check_vma=False,
    )
```

profile of v0, /device:TPU:0, one launch (start us, length us, event | category | flops | bytes accessed | tf_op | source)
XLA Modules:
  0.0 392.7 jit_solution(6487991175751841340)
XLA Ops:
  7.2 0.0 copy-start
  7.2 0.0 all-gather.3.cloned.1.call-start
  7.2 0.7 all-gather.3.cloned.1.call-update
  7.9 0.0 all-gather.5.cloned.1.call-start
  8.0 0.7 all-gather.5.cloned.1.call-update
  8.7 0.0 reduce-scatter.2.cloned.1.call-start
  8.7 0.0 copy-start.3
  8.7 9.1 %copy.10 = f32[2048,1024]{0,1:T(8,128)} copy(f32[2048,1024]{1,0:T(8,128)} %param.6) | data formatting | bytes 16777216 | tf_op args[0]
  17.9 0.0 copy-done.3
  17.9 66.5 %all-gather.3.cloned.1.call-done = f32[1024,1024]{1,0:T(8,128)} async-done(((f32[128,1024]{1,0:T(8,128)}), f32[1024,1024]{1,0:T(8,128)}) %all-gather.3.cloned.1.call-update) | async-done | bytes 4194320 | tf_op jit(solution)/shard_map/all_gather | solution.py:19
  84.4 8.6 %gather_fusion = f32[1024,1024]{1,0:T(8,128)} fusion(f32[1024,1024]{1,0:T(8,128)} %all-gather.3.cloned.1.call-done, s32[1024]{0:T(1024)S(1)} %fusion.32), kind=kCustom, calls=%fused_computation | custom fusion | bytes 8392704 | tf_op jit(solution)/shard_map/jit(_take)/gather | solution.py:21
  93.0 17.9 %fusion.5 = f32[1024,1024]{1,0:T(8,128)} fusion(f32[1024,1024]{1,0:T(8,128)} %param.10, f32[1024,1024]{1,0:T(8,128)} %gather_fusion, pred[1024]{0:T(1024)(128)(4,1)S(1)} %compare_and_fusion), kind=kOutput, calls=%fused_computation.8 | convolution fusion | flops 6443499520 | bytes 12583936 | tf_op jit(solution)/shard_map/dot_general | solution.py:10
  110.9 25.2 %all-gather.5.cloned.1.call-done = f32[2048,1024]{0,1:T(8,128)} async-done(((f32[2048,64]{0,1:T(8,128)}), f32[2048,1024]{0,1:T(8,128)}) %all-gather.5.cloned.1.call-update) | async-done | bytes 8388624 | tf_op jit(solution)/shard_map/all_gather | solution.py:20
  136.1 17.8 %bitcast_subtract_fusion = f32[2048,1024]{0,1:T(8,128)S(1)} fusion(f32[2048,1024]{0,1:T(8,128)} %copy.10, f32[1024,1024]{1,0:T(8,128)} %fusion.5, f32[2048,1024]{0,1:T(8,128)} %all-gather.5.cloned.1.call-done), kind=kOutput, calls=%fused_computation.1 | convolution fusion | flops 12886999040 | bytes 29360128 | tf_op jit(solution)/shard_map/dot_general | solution.py:10
  154.0 0.0 copy-start.1
  154.3 0.0 copy-done
  154.3 7.6 %fusion = f32[2048,512]{0,1:T(8,128)S(1)} fusion(f32[1024,512]{1,0:T(8,128)S(1)} %copy-done, f32[2048,1024]{0,1:T(8,128)S(1)} %bitcast_subtract_fusion, s32[2048]{0:T(1024)S(1)} %add_select_fusion, s32[1024]{0:T(1024)S(1)} %add_select_fusion.1), kind=kOutput, calls=%fused_computation.2 | convolution fusion | flops 6446645248 | bytes 14692352 | tf_op jit(solution)/shard_map/dot_general | solution.py:10
  161.9 0.0 copy-done.1
  161.9 3.0 pad_maximum_fusion
  164.9 0.0 reduce-scatter.2.cloned.1.call-update
  164.9 0.0 all-reduce.2.cloned.1.call-start
  165.0 70.5 %reduce-scatter.2.cloned.1.call-done = f32[128,640]{0,1:T(8,128)} async-done(((f32[2048,640]{0,1:T(8,128)}), f32[128,640]{0,1:T(8,128)}) %reduce-scatter.2.cloned.1.call-update) | async-done | bytes 327696 | tf_op jit(solution)/shard_map/reduce_scatter | solution.py:40
  235.5 2.6 fusion.35
  238.1 0.0 all-reduce.2.cloned.1.call-update
  238.1 0.0 slice-start
  238.1 0.0 slice-start.1
  238.1 119.0 %all-reduce.2.cloned.1.call-done = f32[512,512]{1,0:T(8,128)} async-done(((f32[512,512]{1,0:T(8,128)}), f32[512,512]{1,0:T(8,128)}) %all-reduce.2.cloned.1.call-update) | async-done | bytes 1048592 | tf_op jit(solution)/shard_map/psum | solution.py:50
  357.1 0.0 copy-start.2
  357.1 2.7 collective-permute-start
  359.8 9.2 %copy.11 = f32[2048,1024]{1,0:T(8,128)} copy(f32[2048,1024]{0,1:T(8,128)} %copy-done.1) | data formatting | bytes 16777216
  369.1 0.0 slice-done
  369.1 0.8 copy.12
  369.9 0.0 slice-done.1
  369.9 0.7 copy.13
  370.6 13.1 %collective-permute-done = f32[512,512]{1,0:T(8,128)} collective-permute-done((f32[512,512]{1,0:T(8,128)}, f32[512,512]{1,0:T(8,128)}, u32[]{:S(2)}, u32[]{:S(2)}) %collective-permute-start) | collective-permute-done | bytes 1048608 | tf_op jit(solution)/shard_map/ppermute | solution.py:52
  383.7 0.0 copy-done.2
  383.7 2.4 multiply_bitcast_fusion
  (20 shorter events, 0.2 us)
Async XLA Ops:
  7.2 147.1 %copy-start = (f32[1024,512]{1,0:T(8,128)S(1)}, f32[1024,512]{1,0:T(8,128)}, u32[]{:S(2)}) copy-start(f32[1024,512]{1,0:T(8,128)} %param.11) | copy-start | bytes 6291460
  7.2 77.2 %all-gather.3.cloned.1.call-start = ((), (), s32[]{:S(2)}) async-start(), calls=%async_computation.1 | async-start | bytes 4718592 | tf_op jit(solution)/shard_map/all_gather | solution.py:19
  7.9 128.2 %all-gather.5.cloned.1.call-start = ((), (), s32[]{:S(2)}) async-start(), calls=%async_computation.2 | async-start | bytes 8912896 | tf_op jit(solution)/shard_map/all_gather | solution.py:20
  8.7 226.8 %reduce-scatter.2.cloned.1.call-start = ((), (), s32[]{:S(2)}) async-start(), calls=%async_computation.3 | async-start | bytes 5570560 | tf_op jit(solution)/shard_map/reduce_scatter | solution.py:40
  8.7 9.2 %copy-start.3 = (s32[1024]{0:T(1024)S(1)}, s32[1024]{0:T(1024)}, u32[]{:S(2)}) copy-start(s32[1024]{0:T(1024)} %param.9) | copy-start | bytes 12292
  154.0 7.9 %copy-start.1 = (f32[2048,1024]{0,1:T(8,128)}, f32[2048,1024]{0,1:T(8,128)S(1)}, u32[]{:S(2)}) copy-start(f32[2048,1024]{0,1:T(8,128)S(1)} %bitcast_subtract_fusion) | copy-start | bytes 25165828
  164.9 192.2 %all-reduce.2.cloned.1.call-start = ((), (), s32[]{:S(2)}) async-start(), calls=%async_computation.4 | async-start | bytes 2097152 | tf_op jit(solution)/shard_map/psum | solution.py:50
  238.1 131.0 %slice-start = ((f32[128,640]{0,1:T(8,128)}), f32[128,512]{0,1:T(8,128)S(1)}, s32[]{:S(2)}) async-start(f32[128,640]{0,1:T(8,128)} %reduce-scatter.2.cloned.1.call-done), calls=%async_computation.5 | async-start | bytes 524288 | tf_op jit(solution)/shard_map/slice | solution.py:41
  238.1 131.8 %slice-start.1 = ((f32[128,640]{0,1:T(8,128)}), f32[128,128]{0,1:T(8,128)S(1)}, s32[]{:S(2)}) async-start(f32[128,640]{0,1:T(8,128)} %reduce-scatter.2.cloned.1.call-done), calls=%async_computation.6 | async-start | bytes 131072 | tf_op jit(solution)/shard_map/slice | solution.py:42
  357.1 26.6 %copy-start.2 = (f32[512,512]{1,0:T(8,128)S(1)}, f32[512,512]{1,0:T(8,128)}, u32[]{:S(2)}) copy-start(f32[512,512]{1,0:T(8,128)} %all-reduce.2.cloned.1.call-done) | copy-start | bytes 3145732
  357.1 26.6 %collective-permute-start = (f32[512,512]{1,0:T(8,128)}, f32[512,512]{1,0:T(8,128)}, u32[]{:S(2)}, u32[]{:S(2)}) collective-permute-start(f32[512,512]{1,0:T(8,128)} %all-reduce.2.cloned.1.call-done), channel_id=1, source_target_pairs={{0,16},{16,0},{32,48},{48,32},{64,80},{80,64},{96,112},{112,96},{1... | collective-permute-start | bytes 3145736 | tf_op jit(solution)/shard_map/ppermute | solution.py:52
Sparse Core Ops, SparseCore 0:
  10.3 74.0 all-gather.2
  86.1 49.9 all-gather.4
  165.0 70.3 reduce-scatter.1
  238.4 118.7 all-reduce.1
where the time goes:
time: 393 us
  waiting for transfers between devices  296 us (75%)
  matrix products  45.9 us (12%)
  local copies, waits for them, and re-layouts  28.6 us (7%)
  between operations  14 us (4%)
  other arithmetic  5.64 us (1%)
    psum x1, waiting for transfers between devices, body(): gram = lax.psum(gram, 'col')  119 us
    reduce_scatter x1, waiting for transfers between devices, body(): own = lax.psum_scatter(both, 'col', scatter_dimension=0, tiled=True)  70.5 us
    all_gather x1, waiting for transfers between devices, body(): upper_full = lax.all_gather(panel_rows, 'row', axis=0, tiled=True)  66.5 us
    dot_general x3, matrix products, product(): jnp.dot(left, right, precision=lax.Precision.HIGH, preferred_element_type...  43.3 us
    all_gather x1, waiting for transfers between devices, body(): left = lax.all_gather(panel_columns, 'col', axis=1, tiled=True)  25.2 us
    unnamed x12, local copies, waits for them, and re-layouts  20 us
    ppermute x1, waiting for transfers between devices, body(): gram = gram + lax.ppermute(gram, 'row', route)  13.1 us
    gather x1, local copies, waits for them, and re-layouts, body(): upper = jnp.take(upper_full, pivots, axis=0)  8.63 us
  transfers between devices with their start and end apart: 5, of which 5 were waited for; matrix products, arithmetic and copies ran while one was open for 12% of the time, Pallas kernels for 0%

commit v1 on v0

--- a/solution.py
+++ b/solution.py
@@ -4,6 +4,13 @@
 from jax.sharding import PartitionSpec as P
 
 LEAF = 128
+
+
+def swapped_in(shard, axis, d):
+    devices = lax.axis_size(axis)
+    blocks = jnp.stack([shard for _ in range(devices)])
+    blocks = lax.all_to_all(blocks, axis, split_axis=0, concat_axis=0)
+    return jnp.concatenate(blocks, axis=d)
 
 
 def product(left, right):
@@ -17,7 +24,7 @@
     col_index = lax.axis_index("col")
     height, width = front_trailing.shape
     upper_full = lax.all_gather(panel_rows, "row", axis=0, tiled=True)
-    left = lax.all_gather(panel_columns, "col", axis=1, tiled=True)
+    left = swapped_in(panel_columns, "col", 1)
     upper = jnp.take(upper_full, pivots, axis=0)
     weight = product(diag_inverse, upper)
     schur = front_trailing - product(left, weight)

time: 393 us -> 415 us (1.056)
  waiting for transfers between devices: 296 us -> 306 us
  starting transfers between devices: 2.88 us -> 9.43 us
  local copies, waits for them, and re-layouts: 28.6 us -> 34 us
    all_gather x1 -> x0, waiting for transfers between devices: 25.2 us -> none  [body(): left = lax.all_gather(panel_columns, 'col', axis=1, tiled=True)]
    all_gather x1, waiting for transfers between devices: 66.5 us -> 82.3 us  [body(): upper_full = lax.all_gather(panel_rows, 'row', axis=0, tiled=True)]
    all_to_all x0 -> x1, waiting for transfers between devices: none -> 12.9 us  [swapped_in(): blocks = lax.all_to_all(blocks, axis, split_axis=0, concat_axis=0)]
    reduce_scatter x1, waiting for transfers between devices: 70.5 us -> 77.6 us  [body(): own = lax.psum_scatter(both, 'col', scatter_dimension=0, tiled=True)]
    all_to_all x0 -> x1, starting transfers between devices: none -> 6.59 us  [swapped_in(): blocks = lax.all_to_all(blocks, axis, split_axis=0, concat_axis=0)]
    another operation x0 -> x1, local copies, waits for them, and re-layouts: none -> 5.36 us  [swapped_in(): blocks = jnp.stack([shard for _ in range(devices)])]
where the time goes in v1:
time: 415 us
  waiting for transfers between devices  306 us (74%)
  matrix products  45.8 us (11%)
  local copies, waits for them, and re-layouts  34 us (8%)
  between operations  14 us (3%)
  starting transfers between devices  9.43 us (2%)
  other arithmetic  5.64 us (1%)
    psum x1, waiting for transfers between devices, body(): gram = lax.psum(gram, 'col')  119 us
    all_gather x1, waiting for transfers between devices, body(): upper_full = lax.all_gather(panel_rows, 'row', axis=0, tiled=True)  82.3 us
    reduce_scatter x1, waiting for transfers between devices, body(): own = lax.psum_scatter(both, 'col', scatter_dimension=0, tiled=True)  77.6 us
    dot_general x3, matrix products, product(): jnp.dot(left, right, precision=lax.Precision.HIGH, preferred_element_type...  43.2 us
    unnamed x12, local copies, waits for them, and re-layouts  20 us
    ppermute x1, waiting for transfers between devices, body(): gram = gram + lax.ppermute(gram, 'row', route)  13.1 us
    all_to_all x1, waiting for transfers between devices, swapped_in(): blocks = lax.all_to_all(blocks, axis, split_axis=0, concat_axis=0)  12.9 us
    gather x1, local copies, waits for them, and re-layouts, body(): upper = jnp.take(upper_full, pivots, axis=0)  8.6 us
  transfers between devices with their start and end apart: 5, of which 5 were waited for; matrix products, arithmetic and copies ran while one was open for 12% of the time, Pallas kernels for 0%

profile of v1, /device:TPU:0, one launch (start us, length us, event | category | flops | bytes accessed | tf_op | source)
XLA Modules:
  0.0 414.5 jit_solution(6842408788366659100)
XLA Ops:
  7.2 0.0 copy-start
  7.2 0.0 all-gather.2.cloned.1.call-start
  7.2 0.7 all-gather.2.cloned.1.call-update
  7.9 5.4 %stack.2 = f32[16,2048,64]{1,2,0:T(8,128)} broadcast(f32[2048,64]{0,1:T(8,128)} %param.7), dimensions={1,2} | broadcast | bytes 8912896 | tf_op jit(solution)/shard_map/stack | solution.py:11
  13.3 6.6 %all-to-all-start = ((f32[16,2048,64]{1,2,0:T(8,128)}), f32[16,2048,64]{1,2,0:T(8,128)}, u32[]{:S(2)}, u32[]{:S(2)}) async-start(f32[16,2048,64]{1,2,0:T(8,128)} %stack.2), calls=%async_computation | async-start | bytes 16777216 | tf_op jit(solution)/shard_map/all_to_all | solution.py:12
  19.9 0.0 reduce-scatter.2.cloned.1.call-start
  19.9 0.0 copy-start.3
  19.9 9.2 %copy.15 = f32[2048,1024]{0,1:T(8,128)} copy(f32[2048,1024]{1,0:T(8,128)} %param.6) | data formatting | bytes 16777216 | tf_op args[0]
  29.2 0.0 copy-done.3
  29.2 82.3 %all-gather.2.cloned.1.call-done = f32[1024,1024]{1,0:T(8,128)} async-done(((f32[128,1024]{1,0:T(8,128)}), f32[1024,1024]{1,0:T(8,128)}) %all-gather.2.cloned.1.call-update) | async-done | bytes 4194320 | tf_op jit(solution)/shard_map/all_gather | solution.py:26
  111.4 8.6 %gather_fusion = f32[1024,1024]{1,0:T(8,128)} fusion(f32[1024,1024]{1,0:T(8,128)} %all-gather.2.cloned.1.call-done, s32[1024]{0:T(1024)S(1)} %fusion.32), kind=kCustom, calls=%fused_computation | custom fusion | bytes 8392704 | tf_op jit(solution)/shard_map/jit(_take)/gather | solution.py:28
  120.1 17.8 %fusion.5 = f32[1024,1024]{1,0:T(8,128)} fusion(f32[1024,1024]{1,0:T(8,128)} %param.10, f32[1024,1024]{1,0:T(8,128)} %gather_fusion, pred[1024]{0:T(1024)(128)(4,1)S(1)} %compare_and_fusion), kind=kOutput, calls=%fused_computation.8 | convolution fusion | flops 6443499520 | bytes 12583936 | tf_op jit(solution)/shard_map/dot_general | solution.py:17
  137.9 12.9 %all-to-all-done = f32[16,2048,64]{1,2,0:T(8,128)} async-done(((f32[16,2048,64]{1,2,0:T(8,128)}), f32[16,2048,64]{1,2,0:T(8,128)}, u32[]{:S(2)}, u32[]{:S(2)}) %all-to-all-start) | async-done | bytes 8388640 | tf_op jit(solution)/shard_map/all_to_all | solution.py:12
  150.7 17.8 %bitcast_subtract_fusion = f32[2048,1024]{0,1:T(8,128)S(1)} fusion(f32[2048,1024]{0,1:T(8,128)} %copy.15, f32[1024,1024]{1,0:T(8,128)} %fusion.5, f32[2048,1024]{0,1:T(8,128)} %bitcast.1), kind=kOutput, calls=%fused_computation.1 | convolution fusion | flops 12886999040 | bytes 29360128 | tf_op jit(solution)/shard_map/dot_general | solution.py:17
  168.6 0.0 copy-start.1
  168.9 0.0 copy-done
  168.9 7.6 %fusion = f32[2048,512]{0,1:T(8,128)S(1)} fusion(f32[1024,512]{1,0:T(8,128)S(1)} %copy-done, f32[2048,1024]{0,1:T(8,128)S(1)} %bitcast_subtract_fusion, s32[2048]{0:T(1024)S(1)} %add_select_fusion, s32[1024]{0:T(1024)S(1)} %add_select_fusion.1), kind=kOutput, calls=%fused_computation.2 | convolution fusion | flops 6446645248 | bytes 14692352 | tf_op jit(solution)/shard_map/dot_general | solution.py:17
  176.5 0.0 copy-done.1
  176.5 3.0 pad_maximum_fusion
  179.5 0.0 reduce-scatter.2.cloned.1.call-update
  179.5 0.0 all-reduce.2.cloned.1.call-start
  179.6 77.6 %reduce-scatter.2.cloned.1.call-done = f32[128,640]{0,1:T(8,128)} async-done(((f32[2048,640]{0,1:T(8,128)}), f32[128,640]{0,1:T(8,128)}) %reduce-scatter.2.cloned.1.call-update) | async-done | bytes 327696 | tf_op jit(solution)/shard_map/reduce_scatter | solution.py:47
  257.1 2.6 fusion.35
  259.8 0.0 all-reduce.2.cloned.1.call-update
  259.8 0.0 slice-start
  259.8 0.0 slice-start.1
  259.8 119.1 %all-reduce.2.cloned.1.call-done = f32[512,512]{1,0:T(8,128)} async-done(((f32[512,512]{1,0:T(8,128)}), f32[512,512]{1,0:T(8,128)}) %all-reduce.2.cloned.1.call-update) | async-done | bytes 1048592 | tf_op jit(solution)/shard_map/psum | solution.py:57
  379.0 0.0 copy-start.2
  379.0 2.7 collective-permute-start
  381.7 9.2 %copy.16 = f32[2048,1024]{1,0:T(8,128)} copy(f32[2048,1024]{0,1:T(8,128)} %copy-done.1) | data formatting | bytes 16777216
  390.9 0.0 slice-done
  390.9 0.8 copy.17
  391.8 0.0 slice-done.1
  391.8 0.7 copy.18
  392.5 13.1 %collective-permute-done = f32[512,512]{1,0:T(8,128)} collective-permute-done((f32[512,512]{1,0:T(8,128)}, f32[512,512]{1,0:T(8,128)}, u32[]{:S(2)}, u32[]{:S(2)}) %collective-permute-start) | collective-permute-done | bytes 1048608 | tf_op jit(solution)/shard_map/ppermute | solution.py:59
  405.6 0.0 copy-done.2
  405.6 2.4 multiply_bitcast_fusion
  (20 shorter events, 0.2 us)
Async XLA Ops:
  7.2 161.7 %copy-start = (f32[1024,512]{1,0:T(8,128)S(1)}, f32[1024,512]{1,0:T(8,128)}, u32[]{:S(2)}) copy-start(f32[1024,512]{1,0:T(8,128)} %param.11) | copy-start | bytes 6291460
  7.2 104.3 %all-gather.2.cloned.1.call-start = ((), (), s32[]{:S(2)}) async-start(), calls=%async_computation.2 | async-start | bytes 4718592 | tf_op jit(solution)/shard_map/all_gather | solution.py:26
  13.3 137.5 %all-to-all-start = ((f32[16,2048,64]{1,2,0:T(8,128)}), f32[16,2048,64]{1,2,0:T(8,128)}, u32[]{:S(2)}, u32[]{:S(2)}) async-start(f32[16,2048,64]{1,2,0:T(8,128)} %stack.2), calls=%async_computation | async-start | bytes 16777216 | tf_op jit(solution)/shard_map/all_to_all | solution.py:12
  19.9 237.3 %reduce-scatter.2.cloned.1.call-start = ((), (), s32[]{:S(2)}) async-start(), calls=%async_computation.3 | async-start | bytes 5570560 | tf_op jit(solution)/shard_map/reduce_scatter | solution.py:47
  19.9 9.2 %copy-start.3 = (s32[1024]{0:T(1024)S(1)}, s32[1024]{0:T(1024)}, u32[]{:S(2)}) copy-start(s32[1024]{0:T(1024)} %param.9) | copy-start | bytes 12292
  168.6 7.9 %copy-start.1 = (f32[2048,1024]{0,1:T(8,128)}, f32[2048,1024]{0,1:T(8,128)S(1)}, u32[]{:S(2)}) copy-start(f32[2048,1024]{0,1:T(8,128)S(1)} %bitcast_subtract_fusion) | copy-start | bytes 25165828
  179.5 199.4 %all-reduce.2.cloned.1.call-start = ((), (), s32[]{:S(2)}) async-start(), calls=%async_computation.4 | async-start | bytes 2097152 | tf_op jit(solution)/shard_map/psum | solution.py:57
  259.8 131.1 %slice-start = ((f32[128,640]{0,1:T(8,128)}), f32[128,512]{0,1:T(8,128)S(1)}, s32[]{:S(2)}) async-start(f32[128,640]{0,1:T(8,128)} %reduce-scatter.2.cloned.1.call-done), calls=%async_computation.5 | async-start | bytes 524288 | tf_op jit(solution)/shard_map/slice | solution.py:48
  259.8 132.0 %slice-start.1 = ((f32[128,640]{0,1:T(8,128)}), f32[128,128]{0,1:T(8,128)S(1)}, s32[]{:S(2)}) async-start(f32[128,640]{0,1:T(8,128)} %reduce-scatter.2.cloned.1.call-done), calls=%async_computation.6 | async-start | bytes 131072 | tf_op jit(solution)/shard_map/slice | solution.py:49
  379.0 26.6 %copy-start.2 = (f32[512,512]{1,0:T(8,128)S(1)}, f32[512,512]{1,0:T(8,128)}, u32[]{:S(2)}) copy-start(f32[512,512]{1,0:T(8,128)} %all-reduce.2.cloned.1.call-done) | copy-start | bytes 3145732
  379.0 26.6 %collective-permute-start = (f32[512,512]{1,0:T(8,128)}, f32[512,512]{1,0:T(8,128)}, u32[]{:S(2)}, u32[]{:S(2)}) collective-permute-start(f32[512,512]{1,0:T(8,128)} %all-reduce.2.cloned.1.call-done), channel_id=1, source_target_pairs={{0,16},{16,0},{32,48},{48,32},{64,80},{80,64},{96,112},{112,96},{1... | collective-permute-start | bytes 3145736 | tf_op jit(solution)/shard_map/ppermute | solution.py:59
Sparse Core Ops, SparseCore 0:
  10.3 101.0 all-gather.1
  179.6 77.4 reduce-scatter.1
  260.2 118.7 all-reduce.1
